TPU v7x, 128 devices: a whole 4x4x4 slice. The times are simulated.
128 devices in a mesh: user: 16 (over y_lo, x, core), item: 8 (over z, y_hi).
Axes of the slice: x: 4, y: 4 (y_hi: 2, y_lo: 2; y = y_hi * 2 + y_lo), z: 4, core: 2. Of those that a mesh axis runs over, the one named last changes fastest.
Arguments:
- u_factors: float32 [262144, 256], P(('user', 'item')), may hold values from -1.5 to 1.5
- v_factors: float32 [32768, 256], P(('item', 'user')), may hold values from -1.5 to 1.5
- ratings: bfloat16 [16, 8, 2, 224, 128, 128], P('user', 'item'), may hold values from -6 to 6
- tile_rows: int32 [16, 8, 2, 224], P('user', 'item'), may hold values from 0 to 15, as said below
- tile_cols: int32 [16, 8, 2, 224], P('user', 'item'), may hold values from 0 to 31
- tile_counts: int32 [16, 8, 2], P('user', 'item'), may hold values from 28 to 224, as said below
- u_noise: bfloat16 [2, 262144, 256], P(None, ('user', 'item')), may hold values from -6 to 6
- v_noise: bfloat16 [2, 32768, 256], P(None, ('item', 'user')), may hold values from -6 to 6
Outputs:
- new_users: float32 [262144, 256], P(('user', 'item'))
- new_items: float32 [32768, 256], P(('item', 'user'))
Inputs may be any that keep to these rules, and one draw needn't show every extreme that they name: Within one list of a block and sub-epoch the (tile_rows, tile_cols) pairs are distinct over all 224 slots. `tile_counts`: some list in every draw is full and some has the smallest count.
All inputs are finite; a program needn't handle non-finite values.
Results may differ from a plain program's by a relative error of at most 0.00115.
Values may be sent and summed in bfloat16 or wider, within the bound.
A program may use at most 128 MiB of HBM per device.

v0:
```python
import math

import jax
import jax.numpy as jnp
from jax import lax
from jax.sharding import PartitionSpec as P

HALF_STEP = 0.002
ROOT_STEP = math.sqrt(0.004)
PRIOR = 25.0


def shifted(x, axis, by):
    peers = lax.axis_size(axis)
    return lax.ppermute(x, axis, [(i, (i + by) % peers) for i in range(peers)])


def tile_grads(user_bf, group_bf, rating_list, row_list, col_list, live_count, tile_size):
    width = user_bf.shape[1]
    user_tiles = user_bf.reshape(-1, tile_size, width)
    item_tiles = group_bf.reshape(-1, tile_size, width)
    listed = rating_list.shape[0]
    step_len = math.gcd(listed, 16)

    def advance(position, carry):
        grad_user, grad_item = carry
        first = position * step_len
        ratings_now = lax.dynamic_slice_in_dim(rating_list, first, step_len, 0)
        rows_now = lax.dynamic_slice_in_dim(row_list, first, step_len, 0)
        cols_now = lax.dynamic_slice_in_dim(col_list, first, step_len, 0)
        live = first + jnp.arange(step_len) < live_count
        user_part = user_tiles[rows_now]
        item_part = item_tiles[cols_now]
        predicted = jnp.einsum(
            "tak,tbk->tab", user_part, item_part, preferred_element_type=jnp.float32
        )
        misfit = jnp.where(
            live[:, None, None], ratings_now.astype(jnp.float32) - predicted, 0.0
        ).astype(jnp.bfloat16)
        grad_user = grad_user.at[rows_now].add(
            jnp.einsum("tab,tbk->tak", misfit, item_part, preferred_element_type=jnp.float32)
        )
        grad_item = grad_item.at[cols_now].add(
            jnp.einsum("tab,tak->tbk", misfit, user_part, preferred_element_type=jnp.float32)
        )
        return (grad_user, grad_item)

    steps_needed = (live_count + step_len - 1) // step_len
    initial = (jnp.zeros(user_tiles.shape, jnp.float32), jnp.zeros(item_tiles.shape, jnp.float32))
    grad_user, grad_item = lax.fori_loop(0, steps_needed, advance, initial)
    return (grad_user.reshape(user_bf.shape), grad_item.reshape(group_bf.shape))


def body(u_factors, v_factors, ratings, tile_rows, tile_cols, tile_counts, u_noise, v_noise):
    tile_size = ratings.shape[-1]
    sections = ratings.shape[2]
    power = float(lax.axis_size("item"))
    user_master = u_factors
    item_master = v_factors
    for section in range(sections):
        group_bf = lax.all_gather(item_master.astype(jnp.bfloat16), "user", axis=0, tiled=True)
        grad_user, grad_item = tile_grads(
            user_master.astype(jnp.bfloat16),
            group_bf,
            ratings[0, 0, section],
            tile_rows[0, 0, section],
            tile_cols[0, 0, section],
            tile_counts[0, 0, section],
            tile_size,
        )
        user_master = (
            user_master
            + HALF_STEP * (power * grad_user - PRIOR * user_master)
            + ROOT_STEP * u_noise[section].astype(jnp.float32)
        )
        owned = lax.psum_scatter(grad_item, "user", scatter_dimension=0, tiled=True)
        item_master = (
            item_master
            + HALF_STEP * (power * owned - PRIOR * item_master)
            + ROOT_STEP * v_noise[section].astype(jnp.float32)
        )
        if section + 1 < sections:
            item_master = shifted(item_master, "item", 1)
    item_master = shifted(item_master, "item", 1 - sections)
    return (user_master, item_master)


def solution(mesh):
    placed = (
        P(("user", "item"), None),
        P(("item", "user"), None),
        P("user", "item", None, None, None, None),
        P("user", "item", None, None),
        P("user", "item", None, None),
        P("user", "item", None),
        P(None, ("user", "item"), None),
        P(None, ("item", "user"), None),
    )
    return jax.shard_map(
        body,
        mesh=mesh,
        in_specs=placed,
        out_specs=(P(("user", "item"), None), P(("item", "user"), None)),
        check_vma=False,
    )
```

profile of v0, /device:TPU:0, one launch (start us, length us, event | category | flops | bytes accessed | tf_op | source)
XLA Modules:
  0.0 737.3 jit_solution(3230012545555572059)
XLA Ops:
  7.2 1.6 convert_element_type.41
  8.9 1.3 fusion.11
  10.8 1.7 convert_element_type.40
  12.6 10.7 %slice_bitcast_fusion.1 = (bf16[224,128,128]{2,1,0:T(8,128)(2,1)}, bf16[224,128,128]{2,1,0:T(8,128)(2,1)}) fusion(bf16[1,1,2,224,128,128]{5,4,3,2,1,0:T(8,128)(2,1)} %param.14), kind=kLoop, calls=%fused_computation.25 | loop fusion | bytes 29360128 | tf_op jit(solution)/shard_map/squeeze | solution.py:65
  23.3 23.1 %all-gather.3.cloned.1.call-done = bf16[4096,256]{1,0:T(8,128)(2,1)} async-done(((bf16[256,256]{1,0:T(8,128)(2,1)}), bf16[4096,256]{1,0:T(8,128)(2,1)}) %all-gather.3.cloned.1.call-update) | async-done | bytes 2097168 | tf_op jit(solution)/shard_map/all_gather | solution.py:61
  46.4 2.5 broadcast.76.clone
  48.9 1.5 broadcast.75.clone
  50.4 54.5 %while.24 = (s32[]{:T(128)}, f32[16,128,256]{2,1,0:T(8,128)}, f32[32,128,256]{2,1,0:T(8,128)}, s32[]{:T(128)}, s32[224]{0:T(256)S(1)}, /*index=5*/s32[]{:T(128)}...) while((s32[]{:T(128)}, f32[16,128,256]{2,1,0:T(8,128)}, ...), condition=%wide.region_3.4_spmd, body=%wide.region_0.3_spmd.sunk | while | flops 404752512 | bytes 37757876 | solution.py:50
  51.4 2.2 gather_fusion.1
  54.2 1.5 fusion.52
  55.7 1.8 fusion.54
  57.5 5.3 scatter_fusion.1
  62.8 1.5 fusion.53
  64.2 4.4 scatter_fusion
  69.6 2.2 gather_fusion.1
  72.4 1.5 fusion.52
  73.9 1.8 fusion.54
  75.7 5.3 scatter_fusion.1
  81.0 1.5 fusion.53
  82.4 4.3 scatter_fusion
  87.8 2.2 gather_fusion.1
  90.5 1.5 fusion.52
  92.0 1.8 fusion.54
  93.9 5.2 scatter_fusion.1
  99.1 1.5 fusion.53
  100.6 4.3 scatter_fusion
  105.0 264.2 %reduce-scatter.3.cloned.1.call-done = f32[256,256]{1,0:T(8,128)} async-done(((f32[4096,256]{1,0:T(8,128)}), f32[256,256]{1,0:T(8,128)}) %reduce-scatter.3.cloned.1.call-update) | async-done | bytes 262160 | tf_op jit(solution)/shard_map/reduce_scatter | solution.py:76
  369.2 1.0 bitcast_add_fusion.3
  370.2 2.8 collective-permute-start
  373.0 7.3 collective-permute-done
  381.9 1.4 copy-done.9
  385.2 26.6 %all-gather.5.cloned.1.call-done = bf16[4096,256]{1,0:T(8,128)(2,1)} async-done(((bf16[256,256]{1,0:T(8,128)(2,1)}), bf16[4096,256]{1,0:T(8,128)(2,1)}) %all-gather.5.cloned.1.call-update) | async-done | bytes 2097168 | tf_op jit(solution)/shard_map/all_gather | solution.py:61
  411.8 2.5 broadcast.76
  414.3 1.5 broadcast.75
  415.9 72.8 %while.25 = (s32[]{:T(128)}, f32[16,128,256]{2,1,0:T(8,128)}, f32[32,128,256]{2,1,0:T(8,128)}, s32[]{:T(128)}, s32[224]{0:T(256)S(1)}, /*index=5*/s32[]{:T(128)}...) while((s32[]{:T(128)}, f32[16,128,256]{2,1,0:T(8,128)}, ...), condition=%wide.region_8.9_spmd, body=%wide.region_5.8_spmd.sunk | while | flops 404752512 | bytes 37757876 | solution.py:50
  416.9 2.2 gather_fusion.3
  419.7 1.5 fusion.61
  421.2 1.8 fusion.63
  423.0 5.3 scatter_fusion.3
  428.3 1.5 fusion.62
  429.7 4.4 scatter_fusion.2
  435.1 2.2 gather_fusion.3
  438.0 1.5 fusion.61
  439.5 1.8 fusion.63
  441.3 5.3 scatter_fusion.3
  446.6 1.5 fusion.62
  448.0 4.4 scatter_fusion.2
  453.4 2.2 gather_fusion.3
  456.2 1.5 fusion.61
  457.8 1.8 fusion.63
  459.6 5.2 scatter_fusion.3
  464.7 1.5 fusion.62
  466.2 4.4 scatter_fusion.2
  471.5 2.2 gather_fusion.3
  474.4 1.5 fusion.61
  475.9 1.8 fusion.63
  477.7 5.2 scatter_fusion.3
  482.9 1.5 fusion.62
  484.3 4.4 scatter_fusion.2
  488.7 1.6 copy-done.2
  490.3 1.6 broadcast_multiply_fusion
  491.9 226.2 %reduce-scatter.5.cloned.1.call-done = f32[256,256]{1,0:T(8,128)} async-done(((f32[4096,256]{1,0:T(8,128)}), f32[256,256]{1,0:T(8,128)}) %reduce-scatter.5.cloned.1.call-update) | async-done | bytes 262160 | tf_op jit(solution)/shard_map/reduce_scatter | solution.py:76
  719.1 5.2 collective-permute-start.1
  724.3 5.8 bitcast_add_fusion
  (111 shorter events, 15.7 us)
Async XLA Ops:
  7.2 5.4 copy-start.14
  7.2 5.4 copy-start.15
  7.2 39.2 %all-gather.3.cloned.1.call-start = ((), (), s32[]{:S(2)}) async-start(), calls=%async_computation.2 | async-start | bytes 2228224 | tf_op jit(solution)/shard_map/all_gather | solution.py:61
  8.9 360.3 %reduce-scatter.3.cloned.1.call-start = ((), (), s32[]{:S(2)}) async-start(), calls=%async_computation.3 | async-start | bytes 4456448 | tf_op jit(solution)/shard_map/reduce_scatter | solution.py:76
  50.4 1.0 copy-start.4
  55.7 1.9 copy-start
  64.2 4.4 copy-start.5
  68.6 1.0 copy-start.4
  73.8 1.9 copy-start
  82.4 4.3 copy-start.5
  86.8 1.0 copy-start.4
  92.0 1.9 copy-start
  100.6 4.3 copy-start.5
  104.9 264.3 %copy-start.11 = (f32[256,256]{1,0:T(8,128)S(1)}, f32[256,256]{1,0:T(8,128)}, u32[]{:S(2)}) copy-start(f32[256,256]{1,0:T(8,128)} %param.13) | copy-start | bytes 786436
  104.9 264.3 %copy-start.12 = (bf16[2,256,256]{2,1,0:T(8,128)(2,1)S(1)}, bf16[2,256,256]{2,1,0:T(8,128)(2,1)}, u32[]{:S(2)}) copy-start(bf16[2,256,256]{2,1,0:T(8,128)(2,1)} %param.19) | copy-start | bytes 786436
  104.9 276.8 %copy-start.3 = (f32[16,128,256]{2,1,0:T(8,128)S(1)}, f32[16,128,256]{2,1,0:T(8,128)}, u32[]{:S(2)}) copy-start(f32[16,128,256]{2,1,0:T(8,128)} %get-tuple-element.110) | copy-start | bytes 6291460
  104.9 306.9 %all-gather.5.cloned.1.call-start = ((), (), s32[]{:S(2)}) async-start(), calls=%async_computation.4 | async-start | bytes 2228224 | tf_op jit(solution)/shard_map/all_gather | solution.py:61
  370.2 10.1 %collective-permute-start = (f32[256,256]{1,0:T(8,128)S(1)}, f32[256,256]{1,0:T(8,128)S(1)}, u32[]{:S(2)}, u32[]{:S(2)}) collective-permute-start(f32[256,256]{1,0:T(8,128)S(1)} %bitcast_add_fusion.3), channel_id=1, source_target_pairs={{0,1},{1,2},{2,3},{3,4},{4,5},{5,6},{6,7},{7,0},{8,9},{9,10},{10,1... | collective-permute-start | bytes 786440 | tf_op jit(solution)/shard_map/ppermute | solution.py:15
  381.0 337.1 %reduce-scatter.5.cloned.1.call-start = ((), (), s32[]{:S(2)}) async-start(), calls=%async_computation.5 | async-start | bytes 4456448 | tf_op jit(solution)/shard_map/reduce_scatter | solution.py:76
  381.7 2.4 copy-start.8
  381.7 3.0 copy-start.10
  381.8 1.4 copy-start.9
  415.9 1.0 copy-start.6
  421.2 1.8 copy-start.1
  429.7 4.4 copy-start.7
  434.1 1.0 copy-start.6
  439.4 1.8 copy-start.1
  448.0 4.4 copy-start.7
  452.4 1.0 copy-start.6
  457.7 1.8 copy-start.1
  466.2 4.4 copy-start.7
  470.6 1.0 copy-start.6
  475.9 1.8 copy-start.1
  484.3 4.4 copy-start.7
  488.7 1.6 copy-start.2
  490.3 227.8 %copy-start.13 = (bf16[2,256,256]{2,1,0:T(8,128)(2,1)S(1)}, bf16[2,256,256]{2,1,0:T(8,128)(2,1)}, u32[]{:S(2)}) copy-start(bf16[2,256,256]{2,1,0:T(8,128)(2,1)} %param.19) | copy-start | bytes 786436
  719.1 10.9 %collective-permute-start.1 = (f32[256,256]{1,0:T(8,128)S(1)}, f32[256,256]{1,0:T(8,128)S(1)}, u32[]{:S(2)}, u32[]{:S(2)}) collective-permute-start(f32[256,256]{1,0:T(8,128)S(1)} %bitcast_add_fusion.2), channel_id=1, source_target_pairs={{0,7},{1,0},{2,1},{3,2},{4,3},{5,4},{6,5},{7,6},{8,15},{9,8},{10,9... | collective-permute-start | bytes 786440 | tf_op jit(solution)/shard_map/ppermute | solution.py:15
Sparse Core Ops, SparseCore 0:
  10.3 36.1 all-gather.2
  105.1 264.0 reduce-scatter.2
  381.1 30.6 all-gather.4
  488.8 229.1 reduce-scatter.4
where the time goes:
time: 741 us; the launch traced here: 737 us
  waiting for transfers between devices  547 us (74%)
  other arithmetic  86 us (12%)
  local copies, waits for them, and re-layouts  46.8 us (6%)
  matrix products  33.4 us (5%)
  between operations  15.1 us (2%)
  starting transfers between devices  8.14 us (1%)
    reduce_scatter x2, waiting for transfers between devices, body(): owned = lax.psum_scatter(grad_item, 'user', scatter_dimension=0, tiled=True)  490 us
    all_gather x2, waiting for transfers between devices, body(): lax.all_gather(item_master.astype(jnp.bfloat16), 'user', axis=0, tiled=True)  49.7 us
    scatter-add x7, other arithmetic, advance(): grad_item.at[cols_now]  36.6 us
    scatter-add x7, other arithmetic, advance(): grad_user.at[rows_now]  30.5 us
    gather x7, local copies, waits for them, and re-layouts, advance(): item_part = item_tiles[cols_now]  15.4 us
  transfers between devices with their start and end apart: 6, of which 5 were waited for; matrix products, arithmetic and copies ran while one was open for 3% of the time, Pallas kernels for 0%

commit v1 on v0

v1 whole, which is shorter than its diff:
```python
import functools
import math

import jax
import jax.numpy as jnp
from jax import lax
from jax.experimental import pallas as pl
from jax.experimental.pallas import tpu as pltpu
from jax.sharding import PartitionSpec as P

HALF_STEP = 0.002
ROOT_STEP = math.sqrt(0.004)
PRIOR = 25.0
GROUP = 8


def shifted(x, axis, by):
    peers = lax.axis_size(axis)
    return lax.ppermute(x, axis, [(i, (i + by) % peers) for i in range(peers)])


def tile_kernel(section, rows, cols, count, user_ref, item_ref, rating_ref, gu_ref, gv_ref, misfit_ref):
    gu_ref[...] = jnp.zeros_like(gu_ref)
    gv_ref[...] = jnp.zeros_like(gv_ref)
    live = count[section]

    def predict(step, slot):
        for q in range(GROUP):
            t = step * GROUP + q
            predicted = lax.dot_general(
                user_ref[rows[section, t]],
                item_ref[cols[section, t]],
                (((1,), (1,)), ((), ())),
                preferred_element_type=jnp.float32,
            )
            misfit = jnp.where(t < live, rating_ref[0, t].astype(jnp.float32) - predicted, 0.0)
            misfit_ref[slot * GROUP + q] = misfit.astype(jnp.bfloat16)

    def grads(step, slot):
        parts = []
        for q in range(GROUP):
            t = step * GROUP + q
            misfit = misfit_ref[slot * GROUP + q]
            parts.append(
                (
                    jnp.dot(misfit, item_ref[cols[section, t]], preferred_element_type=jnp.float32),
                    lax.dot_general(
                        misfit,
                        user_ref[rows[section, t]],
                        (((0,), (0,)), ((), ())),
                        preferred_element_type=jnp.float32,
                    ),
                )
            )
        for q in range(GROUP):
            t = step * GROUP + q
            gu_ref[rows[section, t]] += parts[q][0]
            gv_ref[cols[section, t]] += parts[q][1]

    steps = (live + GROUP - 1) // GROUP
    predict(0, 0)

    def advance(step, _):
        slot = lax.rem(step, 2)
        grads(step, slot)
        predict(jnp.minimum(step + 1, steps - 1), 1 - slot)
        return 0

    lax.fori_loop(0, steps, advance, 0)


def tile_grads(section, user_bf, group_bf, ratings, rows, cols, counts):
    tile = ratings.shape[-1]
    listed = ratings.shape[1]
    width = user_bf.shape[1]
    user_tiles = user_bf.reshape(-1, tile, width)
    item_tiles = group_bf.reshape(-1, tile, width)
    grad_user, grad_item = pl.pallas_call(
        functools.partial(tile_kernel, section),
        grid=(1,),
        out_shape=(
            jax.ShapeDtypeStruct(user_tiles.shape, jnp.float32),
            jax.ShapeDtypeStruct(item_tiles.shape, jnp.float32),
        ),
        in_specs=[
            pl.BlockSpec(memory_space=pltpu.SMEM),
            pl.BlockSpec(memory_space=pltpu.SMEM),
            pl.BlockSpec(memory_space=pltpu.SMEM),
            pl.BlockSpec(user_tiles.shape, lambda i: (0, 0, 0), pipeline_mode=pl.Buffered(1)),
            pl.BlockSpec(item_tiles.shape, lambda i: (0, 0, 0), pipeline_mode=pl.Buffered(1)),
            pl.BlockSpec((1, listed, tile, tile), lambda i: (section, 0, 0, 0), pipeline_mode=pl.Buffered(1)),
        ],
        out_specs=(
            pl.BlockSpec(user_tiles.shape, lambda i: (0, 0, 0)),
            pl.BlockSpec(item_tiles.shape, lambda i: (0, 0, 0)),
        ),
        scratch_shapes=[pltpu.VMEM((2 * GROUP, tile, tile), jnp.bfloat16)],
        compiler_params=pltpu.CompilerParams(vmem_limit_bytes=48 * 1024 * 1024),
    )(rows, cols, counts, user_tiles, item_tiles, ratings)
    return grad_user.reshape(user_bf.shape), grad_item.reshape(group_bf.shape)


def body(u_factors, v_factors, ratings, tile_rows, tile_cols, tile_counts, u_noise, v_noise):
    sections = ratings.shape[2]
    power = float(lax.axis_size("item"))
    user_master = u_factors
    item_master = v_factors
    for section in range(sections):
        group_bf = lax.all_gather(item_master.astype(jnp.bfloat16), "user", axis=0, tiled=True)
        grad_user, grad_item = tile_grads(
            section,
            user_master.astype(jnp.bfloat16),
            group_bf,
            ratings[0, 0],
            tile_rows[0, 0],
            tile_cols[0, 0],
            tile_counts[0, 0],
        )
        user_master = (
            user_master
            + HALF_STEP * (power * grad_user - PRIOR * user_master)
            + ROOT_STEP * u_noise[section].astype(jnp.float32)
        )
        owned = lax.psum_scatter(grad_item, "user", scatter_dimension=0, tiled=True)
        item_master = (
            item_master
            + HALF_STEP * (power * owned - PRIOR * item_master)
            + ROOT_STEP * v_noise[section].astype(jnp.float32)
        )
        if section + 1 < sections:
            item_master = shifted(item_master, "item", 1)
    item_master = shifted(item_master, "item", 1 - sections)
    return (user_master, item_master)


def solution(mesh):
    placed = (
        P(("user", "item"), None),
        P(("item", "user"), None),
        P("user", "item", None, None, None, None),
        P("user", "item", None, None),
        P("user", "item", None, None),
        P("user", "item", None),
        P(None, ("user", "item"), None),
        P(None, ("item", "user"), None),
    )
    return jax.shard_map(
        body,
        mesh=mesh,
        in_specs=placed,
        out_specs=(P(("user", "item"), None), P(("item", "user"), None)),
        check_vma=False,
    )
```

time: 741 us -> 286 us (0.39)
  waiting for transfers between devices: 547 us -> 212 us
  other arithmetic: 86 us -> 14.1 us
  local copies, waits for them, and re-layouts: 46.8 us -> 6.72 us
  matrix products: 33.4 us -> 0 us
  Pallas kernels: 0 us -> 29.2 us
    reduce_scatter x2, waiting for transfers between devices: 490 us -> 142 us  [body(): owned = lax.psum_scatter(grad_item, 'user', scatter_dimension=0, tiled=True)]
    scatter-add x14 -> x0, other arithmetic: 67.1 us -> none  [the longest x7 36.6 us: advance(): grad_item.at[cols_now]]
    dot_general x21 -> x0, matrix products: 33.4 us -> none  [the longest x7 12.8 us: advance(): jnp.einsum('tab,tak->tbk', misfit, user_part, preferred_element_type=jnp....]
    pallas_call x0 -> x2, Pallas kernels: none -> 29.2 us  [tile_grads(): pl.pallas_call(functools.partial(tile_kernel, section), grid=(1,), out_sh...]
    gather x14 -> x0, local copies, waits for them, and re-layouts: 19.7 us -> none  [the longest x7 15.4 us: advance(): item_part = item_tiles[cols_now]]
    all_gather x2, waiting for transfers between devices: 49.7 us -> 63.1 us  [body(): lax.all_gather(item_master.astype(jnp.bfloat16), 'user', axis=0, tiled=True)]
    squeeze x1 -> x0, local copies, waits for them, and re-layouts: 10.7 us -> none  [body(): ratings[0, 0, section]]
    another operation x4 -> x0, local copies, waits for them, and re-layouts: 8.08 us -> none
where the time goes in v1:
time: 286 us; the launch traced here: 284 us
  waiting for transfers between devices  212 us (74%)
  Pallas kernels  29.2 us (10%)
  other arithmetic  14.1 us (5%)
  between operations  13.9 us (5%)
  starting transfers between devices  8.14 us (3%)
  local copies, waits for them, and re-layouts  6.72 us (2%)
    reduce_scatter x2, waiting for transfers between devices, body(): owned = lax.psum_scatter(grad_item, 'user', scatter_dimension=0, tiled=True)  142 us
    all_gather x2, waiting for transfers between devices, body(): lax.all_gather(item_master.astype(jnp.bfloat16), 'user', axis=0, tiled=True)  63.1 us
    pallas_call x2, Pallas kernels, tile_grads(): pl.pallas_call(functools.partial(tile_kernel, section), grid=(1,), out_sh...  29.2 us
    ppermute x2, starting transfers between devices, shifted(): return lax.ppermute(x, axis, [(i, (i + by) % peers) for i in range(peers)])  7.97 us
    ppermute x2, waiting for transfers between devices, shifted(): return lax.ppermute(x, axis, [(i, (i + by) % peers) for i in range(peers)])  7.07 us
    unnamed x23, local copies, waits for them, and re-layouts  6.72 us
    add x1, other arithmetic, body(): user_master + HALF_STEP * (power * grad_user - PRIOR * user_master)  5.75 us
  transfers between devices with their start and end apart: 6, of which 5 were waited for; matrix products, arithmetic and copies ran while one was open for 3% of the time, Pallas kernels for 0%

profile of v1, /device:TPU:0, one launch (start us, length us, event | category | flops | bytes accessed | tf_op | source)
XLA Modules:
  0.0 284.4 jit_solution(8391538505369397192)
XLA Ops:
  7.2 0.0 copy-start.4
  7.2 0.0 copy-start.3
  7.2 0.0 copy-start.2
  7.2 0.0 all-gather.3.cloned.1.call-start
  7.2 1.6 convert_element_type.29
  8.9 0.0 all-gather.3.cloned.1.call-update
  8.9 0.0 reduce-scatter.3.cloned.1.call-start
  8.9 1.7 convert_element_type.28
  10.6 35.8 %all-gather.3.cloned.1.call-done = bf16[4096,256]{1,0:T(8,128)(2,1)} async-done(((bf16[256,256]{1,0:T(8,128)(2,1)}), bf16[4096,256]{1,0:T(8,128)(2,1)}) %all-gather.3.cloned.1.call-update) | async-done | bytes 2097168 | tf_op jit(solution)/shard_map/all_gather | solution.py:109
  46.4 0.0 copy-done.4
  46.4 0.0 copy-done.3
  46.4 0.0 copy-done.2
  46.4 0.0 copy-start.1
  46.4 1.6 copy-done.1
  48.0 17.6 %shard_map.95 = (f32[16,128,256]{2,1,0:T(8,128)S(1)}, f32[32,128,256]{2,1,0:T(8,128)}) custom-call(s32[2,224]{1,0:T(2,128)S(1)} %bitcast.46, s32[2,224]{1,0:T(2,128)S(1)} %bitcast.48, s32[2]{0:T(128)S(1)} %bitcast.50, bf16[16,128,256]{2,1,0:T(8,128)(2,1)S(1)} %bitcast.42, bf16[32,128,256]{2,1,0:T(8,128)(2,1)S(1)} %bitcast.45, bf16[2,224,128,128]{3,2,1,0:T(8,128)(2,1)} %bitcast.52), custom_call_target="tpu_custom_call" | custom-call | tf_op jit(solution)/shard_map/pallas_call | solution.py:78
  65.6 0.0 copy-start.8
  65.6 0.0 copy-start.9
  65.6 0.0 reduce-scatter.3.cloned.1.call-update
  65.6 0.0 all-gather.5.cloned.1.call-start
  65.7 69.4 %reduce-scatter.3.cloned.1.call-done = f32[256,256]{1,0:T(8,128)} async-done(((f32[4096,256]{1,0:T(8,128)}), f32[256,256]{1,0:T(8,128)}) %reduce-scatter.3.cloned.1.call-update) | async-done | bytes 262160 | tf_op jit(solution)/shard_map/reduce_scatter | solution.py:124
  135.1 0.0 copy-done.8
  135.1 0.0 copy-done.9
  135.1 1.0 bitcast_add_fusion.3
  136.1 3.0 %collective-permute-start = (f32[256,256]{1,0:T(8,128)S(1)}, f32[256,256]{1,0:T(8,128)S(1)}, u32[]{:S(2)}, u32[]{:S(2)}) collective-permute-start(f32[256,256]{1,0:T(8,128)S(1)} %bitcast_add_fusion.3), channel_id=1, source_target_pairs={{0,1},{1,2},{2,3},{3,4},{4,5},{5,6},{6,7},{7,0},{8,9},{9,10},{10,1... | collective-permute-start | bytes 786440 | tf_op jit(solution)/shard_map/ppermute | solution.py:19
  139.1 7.1 %collective-permute-done = f32[256,256]{1,0:T(8,128)S(1)} collective-permute-done((f32[256,256]{1,0:T(8,128)S(1)}, f32[256,256]{1,0:T(8,128)S(1)}, u32[]{:S(2)}, u32[]{:S(2)}) %collective-permute-start) | collective-permute-done | bytes 262176 | tf_op jit(solution)/shard_map/ppermute | solution.py:19
  146.2 0.7 convert_element_type.33
  146.9 0.0 all-gather.5.cloned.1.call-update
  146.9 0.0 reduce-scatter.5.cloned.1.call-start
  146.9 0.0 copy-start.5
  147.0 0.0 copy-start.7
  147.0 0.1 broadcast_multiply_fusion.1
  147.1 0.0 copy-start.6
  147.1 1.3 copy-done.6
  148.5 0.8 copy-done.5
  149.3 0.6 copy-done.7
  149.9 0.5 fusion.4
  150.4 27.3 %all-gather.5.cloned.1.call-done = bf16[4096,256]{1,0:T(8,128)(2,1)} async-done(((bf16[256,256]{1,0:T(8,128)(2,1)}), bf16[4096,256]{1,0:T(8,128)(2,1)}) %all-gather.5.cloned.1.call-update) | async-done | bytes 2097168 | tf_op jit(solution)/shard_map/all_gather | solution.py:109
  177.7 0.0 copy-start
  177.7 1.6 copy-done
  179.3 11.6 %shard_map.96 = (f32[16,128,256]{2,1,0:T(8,128)S(1)}, f32[32,128,256]{2,1,0:T(8,128)}) custom-call(s32[2,224]{1,0:T(2,128)S(1)} %bitcast.47, s32[2,224]{1,0:T(2,128)S(1)} %bitcast.49, s32[2]{0:T(128)S(1)} %bitcast.51, bf16[16,128,256]{2,1,0:T(8,128)(2,1)S(1)} %bitcast.43, bf16[32,128,256]{2,1,0:T(8,128)(2,1)S(1)} %bitcast.44, bf16[2,224,128,128]{3,2,1,0:T(8,128)(2,1)} %bitcast.53), custom_call_target="tpu_custom_call" | custom-call | tf_op jit(solution)/shard_map/pallas_call | solution.py:78
  190.9 0.0 reduce-scatter.5.cloned.1.call-update
  191.0 0.0 copy-start.10
  191.0 1.6 broadcast_multiply_fusion
  192.6 72.9 %reduce-scatter.5.cloned.1.call-done = f32[256,256]{1,0:T(8,128)} async-done(((f32[4096,256]{1,0:T(8,128)}), f32[256,256]{1,0:T(8,128)}) %reduce-scatter.5.cloned.1.call-update) | async-done | bytes 262160 | tf_op jit(solution)/shard_map/reduce_scatter | solution.py:124
  265.4 0.0 copy-done.10
  265.4 1.0 bitcast_add_fusion.2
  266.5 5.0 %collective-permute-start.1 = (f32[256,256]{1,0:T(8,128)S(1)}, f32[256,256]{1,0:T(8,128)S(1)}, u32[]{:S(2)}, u32[]{:S(2)}) collective-permute-start(f32[256,256]{1,0:T(8,128)S(1)} %bitcast_add_fusion.2), channel_id=1, source_target_pairs={{0,7},{1,0},{2,1},{3,2},{4,3},{5,4},{6,5},{7,6},{8,15},{9,8},{10,9... | collective-permute-start | bytes 786440 | tf_op jit(solution)/shard_map/ppermute | solution.py:19
  271.5 5.8 %bitcast_add_fusion = f32[2048,256]{1,0:T(8,128)} fusion(f32[16,128,256]{2,1,0:T(8,128)} %broadcast_multiply_fusion, bf16[2,2048,256]{2,1,0:T(8,128)(2,1)} %param.14, f32[2048,256]{1,0:T(8,128)} %param.8, f32[16,128,256]{2,1,0:T(8,128)} %copy-done.6), kind=kLoop, calls=%fused_computation | loop fusion | flops 7340032 | bytes 10485760 | tf_op jit(solution)/shard_map/add | solution.py:120
  277.2 0.0 collective-permute-done.1
  277.2 0.7 copy.11
Async XLA Ops:
  7.2 39.3 %copy-start.4 = (s32[1,1,2]{2,1,0:T(1,128)S(1)}, s32[1,1,2]{2,1,0:T(1,128)}, u32[]{:S(2)}) copy-start(s32[1,1,2]{2,1,0:T(1,128)} %param.13) | copy-start | bytes 28
  7.2 39.3 %copy-start.3 = (s32[1,1,2,224]{3,2,1,0:T(2,128)S(1)}, s32[1,1,2,224]{3,2,1,0:T(2,128)}, u32[]{:S(2)}) copy-start(s32[1,1,2,224]{3,2,1,0:T(2,128)} %param.12) | copy-start | bytes 5380
  7.2 39.3 %copy-start.2 = (s32[1,1,2,224]{3,2,1,0:T(2,128)S(1)}, s32[1,1,2,224]{3,2,1,0:T(2,128)}, u32[]{:S(2)}) copy-start(s32[1,1,2,224]{3,2,1,0:T(2,128)} %param.11) | copy-start | bytes 5380
  7.2 39.2 %all-gather.3.cloned.1.call-start = ((), (), s32[]{:S(2)}) async-start(), calls=%async_computation.2 | async-start | bytes 2228224 | tf_op jit(solution)/shard_map/all_gather | solution.py:109
  8.9 126.2 %reduce-scatter.3.cloned.1.call-start = ((), (), s32[]{:S(2)}) async-start(), calls=%async_computation.3 | async-start | bytes 4456448 | tf_op jit(solution)/shard_map/reduce_scatter | solution.py:124
  46.4 1.6 copy-start.1
  65.6 69.5 %copy-start.8 = (f32[256,256]{1,0:T(8,128)S(1)}, f32[256,256]{1,0:T(8,128)}, u32[]{:S(2)}) copy-start(f32[256,256]{1,0:T(8,128)} %param.9) | copy-start | bytes 786436
  65.6 69.5 %copy-start.9 = (bf16[2,256,256]{2,1,0:T(8,128)(2,1)S(1)}, bf16[2,256,256]{2,1,0:T(8,128)(2,1)}, u32[]{:S(2)}) copy-start(bf16[2,256,256]{2,1,0:T(8,128)(2,1)} %param.15) | copy-start | bytes 786436
  65.6 112.1 %all-gather.5.cloned.1.call-start = ((), (), s32[]{:S(2)}) async-start(), calls=%async_computation.4 | async-start | bytes 2228224 | tf_op jit(solution)/shard_map/all_gather | solution.py:109
  136.1 10.1 %collective-permute-start = (f32[256,256]{1,0:T(8,128)S(1)}, f32[256,256]{1,0:T(8,128)S(1)}, u32[]{:S(2)}, u32[]{:S(2)}) collective-permute-start(f32[256,256]{1,0:T(8,128)S(1)} %bitcast_add_fusion.3), channel_id=1, source_target_pairs={{0,1},{1,2},{2,3},{3,4},{4,5},{5,6},{6,7},{7,0},{8,9},{9,10},{10,1... | collective-permute-start | bytes 786440 | tf_op jit(solution)/shard_map/ppermute | solution.py:19
  146.9 118.5 %reduce-scatter.5.cloned.1.call-start = ((), (), s32[]{:S(2)}) async-start(), calls=%async_computation.5 | async-start | bytes 4456448 | tf_op jit(solution)/shard_map/reduce_scatter | solution.py:124
  146.9 2.4 copy-start.5
  147.0 3.0 %copy-start.7 = (bf16[2,2048,256]{2,1,0:T(8,128)(2,1)S(1)}, bf16[2,2048,256]{2,1,0:T(8,128)(2,1)}, u32[]{:S(2)}) copy-start(bf16[2,2048,256]{2,1,0:T(8,128)(2,1)} %param.14) | copy-start | bytes 6291460
  147.1 1.3 copy-start.6
  177.7 1.6 copy-start
  191.0 74.5 %copy-start.10 = (bf16[2,256,256]{2,1,0:T(8,128)(2,1)S(1)}, bf16[2,256,256]{2,1,0:T(8,128)(2,1)}, u32[]{:S(2)}) copy-start(bf16[2,256,256]{2,1,0:T(8,128)(2,1)} %param.15) | copy-start | bytes 786436
  266.5 10.7 %collective-permute-start.1 = (f32[256,256]{1,0:T(8,128)S(1)}, f32[256,256]{1,0:T(8,128)S(1)}, u32[]{:S(2)}, u32[]{:S(2)}) collective-permute-start(f32[256,256]{1,0:T(8,128)S(1)} %bitcast_add_fusion.2), channel_id=1, source_target_pairs={{0,7},{1,0},{2,1},{3,2},{4,3},{5,4},{6,5},{7,6},{8,15},{9,8},{10,9... | collective-permute-start | bytes 786440 | tf_op jit(solution)/shard_map/ppermute | solution.py:19
Sparse Core Ops, SparseCore 0:
  10.3 36.1 all-gather.2
  65.7 69.3 reduce-scatter.2
  147.0 30.6 all-gather.4
  191.1 74.2 reduce-scatter.4

commit v2 on v0

v2 whole, which is shorter than its diff:
```python
import math

import jax
import jax.numpy as jnp
from jax import lax
from jax.experimental import pallas as pl
from jax.experimental.pallas import tpu as pltpu
from jax.sharding import PartitionSpec as P

HALF_STEP = 0.002
ROOT_STEP = math.sqrt(0.004)
PRIOR = 25.0
LEVELS = 32767.0
MESH = pl.DeviceIdType.MESH

TILE = 128
WIDTH = 256
BLOCK = 2048
OWNED = 256
CHIPS = 8
ITEM_PEERS = 8
BAND = 256
BANDS = BLOCK // BAND


def visit(o, chip):
    turn = lax.rem(o, 3)
    dx = jnp.where(o < 6, turn + turn // 2, 2)
    dy = jnp.where(o < 6, o // 3, o - 6)
    return lax.rem(chip // 4 + dy, 2) * 4 + lax.rem(lax.rem(chip, 4) + dx, 4)


def whole_kernel(
    power,
    slots,
    u_hbm,
    v_hbm,
    rating_hbm,
    un_hbm,
    vn_hbm,
    uout_hbm,
    vout_hbm,
    ratings_0,
    ratings_1,
    u_now,
    u_bf,
    u_turned,
    grad_u,
    u_noise,
    v_now,
    v_noise,
    v_next,
    v_bf,
    group,
    misfit,
    grad_v,
    from_twin,
    packed,
    scales,
    packed_in,
    scales_in,
    total,
    load_sem,
    ag_send,
    ag_recv,
    twin_send,
    twin_recv,
    q_send,
    q_recv,
    s_send,
    s_recv,
    hop_send,
    hop_recv,
):
    user = lax.axis_index("user")
    item = lax.axis_index("item")
    chip = user // 2
    core = lax.rem(user, 2)
    twin = (chip * 2 + 1 - core, item)
    onward = (user, lax.rem(item + 1, ITEM_PEERS))
    back = (user, lax.rem(item + ITEM_PEERS - 1, ITEM_PEERS))

    def there(o):
        return (visit(o, chip) * 2 + core, item)

    ratings = (ratings_0, ratings_1)
    loads = [
        pltpu.make_async_copy(v_hbm, v_now, load_sem.at[0]),
        pltpu.make_async_copy(u_hbm, u_now, load_sem.at[1]),
        pltpu.make_async_copy(rating_hbm.at[0], ratings_0, load_sem.at[2]),
        pltpu.make_async_copy(un_hbm, u_noise, load_sem.at[3]),
        pltpu.make_async_copy(vn_hbm, v_noise, load_sem.at[4]),
        pltpu.make_async_copy(rating_hbm.at[1], ratings_1, load_sem.at[5]),
    ]
    for load in loads:
        load.start()

    barrier = pltpu.get_barrier_semaphore()
    for peer in [twin, onward, back]:
        pl.semaphore_signal(barrier, inc=1, device_id=peer, device_id_type=MESH)

    def greet(o, _):
        pl.semaphore_signal(barrier, inc=1, device_id=there(o), device_id_type=MESH)
        return 0

    lax.fori_loop(1, CHIPS, greet, 0)
    loads[0].wait()
    group[0, user] = v_now[...].astype(jnp.bfloat16)
    pl.semaphore_wait(barrier, 3 + CHIPS - 1)

    def remote(src, dst, send, recv, device):
        return pltpu.make_async_remote_copy(
            src_ref=src, dst_ref=dst, send_sem=send, recv_sem=recv, device_id=device, device_id_type=MESH
        )

    def ag_copy(s, owner, lane, device):
        at = group.at[s, owner]
        return remote(at, at, ag_send.at[s, lane], ag_recv.at[s, owner], device)

    def spread(s):
        ag_copy(s, user, 0, twin).start()

        def one(o, _):
            ag_copy(s, user, o, there(o)).start()
            return 0

        lax.fori_loop(1, CHIPS, one, 0)

    def twin_copy(s, o):
        return remote(
            grad_v.at[o, 1 - core], from_twin.at[s, o], twin_send.at[s, o], twin_recv.at[s, o], twin
        )

    def q_copy(s, o, slot):
        return remote(packed.at[o], packed_in.at[s, slot], q_send.at[s, o], q_recv.at[s, slot], there(o))

    def s_copy(s, o, slot):
        return remote(scales.at[o], scales_in.at[s, slot], s_send.at[s, o], s_recv.at[s, slot], there(o))

    def prepare(s):
        def one(b, _):
            rows = pl.ds(pl.multiple_of(b * BAND, BAND), BAND)
            now = u_now[rows, :]
            if s > 0:
                now = (
                    now
                    + HALF_STEP * (power * grad_u[rows, :] - PRIOR * now)
                    + ROOT_STEP * u_noise[s - 1, rows, :].astype(jnp.float32)
                )
                u_now[rows, :] = now
            if s < 2:
                u_bf[rows, :] = now.astype(jnp.bfloat16)
                u_turned[:, rows] = now.T.astype(jnp.bfloat16)
                grad_u[rows, :] = jnp.zeros((BAND, WIDTH), jnp.float32)
            return 0

        lax.fori_loop(0, BANDS, one, 0)

    def work(s, o, chip_now, half):
        owner = chip_now * 2 + half
        items = group[s, owner]
        for b in range(BANDS):
            rows = pl.ds(b * BAND, BAND)
            predicted = lax.dot_general(
                u_bf[rows, :], items, (((1,), (1,)), ((), ())), preferred_element_type=jnp.float32
            )
            for i in range(BAND // TILE):
                for j in range(OWNED // TILE):
                    at = slots[s, (b * (BAND // TILE) + i) * 32 + owner * 2 + j]
                    rating = ratings[s][jnp.maximum(at, 0)].astype(jnp.float32)
                    part = predicted[i * TILE : (i + 1) * TILE, j * TILE : (j + 1) * TILE]
                    misfit[pl.ds(b * BAND + i * TILE, TILE), pl.ds(j * TILE, TILE)] = jnp.where(
                        at >= 0, rating - part, 0.0
                    ).astype(jnp.bfloat16)
            grad_u[rows, :] += jnp.dot(misfit[rows, :], items, preferred_element_type=jnp.float32)
        grad_v[o, half] = jnp.dot(u_turned[...], misfit[...], preferred_element_type=jnp.float32)

    def finish(s, o):
        twin_copy(s, o).wait_recv()
        term = grad_v[o, core] + from_twin[s, o]
        peak = jnp.max(jnp.abs(term), axis=0, keepdims=True)
        inverse = jnp.where(peak > 1e-30, LEVELS / jnp.maximum(peak, 1e-30), 0.0)
        packed[o] = jnp.round(term * inverse).astype(jnp.int32).astype(jnp.int16)
        scales[o] = jnp.broadcast_to(peak * (1.0 / LEVELS), (8, OWNED))
        q_copy(s, o, chip).start()
        s_copy(s, o, chip).start()

    def section(s):
        def meet(o, _):
            chip_now = visit(o, chip)
            work(s, o, chip_now, core)

            @pl.when(o + 1 < CHIPS)
            def _():
                owner = visit(o + 1, chip) * 2 + core
                ag_copy(s, owner, 0, twin).wait_recv()
                ag_copy(s, owner, CHIPS + o + 1, twin).start()

            ag_copy(s, chip_now * 2 + 1 - core, 0, twin).wait_recv()
            work(s, o, chip_now, 1 - core)
            twin_copy(s, o).start()

            @pl.when(o > 1)
            def _():
                finish(s, o - 1)

            return 0

        lax.fori_loop(0, CHIPS, meet, 0)
        finish(s, CHIPS - 1)

    def own_sum(s):
        twin_copy(s, 0).wait_recv()
        total[...] = grad_v[0, core] + from_twin[s, 0]

        def add(o, _):
            slot = visit(o, chip)
            q_copy(s, o, slot).wait_recv()
            s_copy(s, o, slot).wait_recv()
            total[...] += packed_in[s, slot].astype(jnp.int32).astype(jnp.float32) * scales_in[s, slot, 0:1, :]
            return 0

        lax.fori_loop(1, CHIPS, add, 0)
        return total[...].T

    def settle(s):
        ag_copy(s, user, 0, twin).wait_send()
        twin_copy(s, 0).wait_send()

        def one(o, _):
            ag_copy(s, user, o, there(o)).wait_send()
            ag_copy(s, user, CHIPS + o, twin).wait_send()
            twin_copy(s, o).wait_send()
            q_copy(s, o, chip).wait_send()
            s_copy(s, o, chip).wait_send()
            return 0

        lax.fori_loop(1, CHIPS, one, 0)

    spread(0)
    loads[1].wait()
    prepare(0)
    loads[2].wait()
    section(0)
    loads[3].wait()
    prepare(1)
    loads[4].wait()
    now = v_now[...]
    now = now + HALF_STEP * (power * own_sum(0) - PRIOR * now) + ROOT_STEP * v_noise[0].astype(jnp.float32)
    v_bf[...] = now.astype(jnp.bfloat16)
    hop = remote(v_bf, group.at[1, user], hop_send.at[0], hop_recv.at[0], onward)
    hop.start()
    v_now[...] = now
    hop_full = remote(v_now, v_next, hop_send.at[1], hop_recv.at[1], onward)
    hop_full.start()
    settle(0)
    hop.wait_recv()

    spread(1)
    loads[5].wait()
    section(1)
    prepare(2)
    store = pltpu.make_async_copy(u_now, uout_hbm, load_sem.at[6])
    store.start()
    hop_full.wait()
    now = v_next[...]
    v_next[...] = (
        now + HALF_STEP * (power * own_sum(1) - PRIOR * now) + ROOT_STEP * v_noise[1].astype(jnp.float32)
    )
    home = remote(v_next, vout_hbm, hop_send.at[2], hop_recv.at[2], back)
    home.start()
    settle(1)
    hop.wait_send()
    store.wait()
    home.wait()


def slot_map(rows, cols, counts):
    sections, listed = rows.shape
    cell = jnp.arange(512, dtype=jnp.int32)[None, :, None]
    slot = jnp.arange(listed, dtype=jnp.int32)
    hit = (rows * 32 + cols)[:, None, :] == cell
    live = (slot[None, :] < counts[:, None])[:, None, :]
    return jnp.max(jnp.where(hit & live, slot[None, None, :], -1), axis=2)


def body(u_factors, v_factors, ratings, tile_rows, tile_cols, tile_counts, u_noise, v_noise):
    slots = slot_map(tile_rows[0, 0], tile_cols[0, 0], tile_counts[0, 0])
    listed = ratings.shape[3]
    power = float(lax.axis_size("item"))
    anywhere = pl.BlockSpec(memory_space=pl.ANY)
    dma = pltpu.SemaphoreType.DMA

    def kernel(*refs):
        whole_kernel(power, *refs)

    return pl.pallas_call(
        kernel,
        out_shape=(
            jax.ShapeDtypeStruct(u_factors.shape, jnp.float32),
            jax.ShapeDtypeStruct(v_factors.shape, jnp.float32),
        ),
        in_specs=[pl.BlockSpec(memory_space=pltpu.SMEM)] + [anywhere] * 5,
        out_specs=(anywhere, anywhere),
        scratch_shapes=[
            pltpu.VMEM((listed, TILE, TILE), jnp.bfloat16),
            pltpu.VMEM((listed, TILE, TILE), jnp.bfloat16),
            pltpu.VMEM((BLOCK, WIDTH), jnp.float32),
            pltpu.VMEM((BLOCK, WIDTH), jnp.bfloat16),
            pltpu.VMEM((WIDTH, BLOCK), jnp.bfloat16),
            pltpu.VMEM((BLOCK, WIDTH), jnp.float32),
            pltpu.VMEM((2, BLOCK, WIDTH), jnp.bfloat16),
            pltpu.VMEM((OWNED, WIDTH), jnp.float32),
            pltpu.VMEM((2, OWNED, WIDTH), jnp.bfloat16),
            pltpu.VMEM((OWNED, WIDTH), jnp.float32),
            pltpu.VMEM((OWNED, WIDTH), jnp.bfloat16),
            pltpu.VMEM((2, 2 * CHIPS, OWNED, WIDTH), jnp.bfloat16),
            pltpu.VMEM((BLOCK, OWNED), jnp.bfloat16),
            pltpu.VMEM((CHIPS, 2, WIDTH, OWNED), jnp.float32),
            pltpu.VMEM((2, CHIPS, WIDTH, OWNED), jnp.float32),
            pltpu.VMEM((CHIPS, WIDTH, OWNED), jnp.int16),
            pltpu.VMEM((CHIPS, 8, OWNED), jnp.float32),
            pltpu.VMEM((2, CHIPS, WIDTH, OWNED), jnp.int16),
            pltpu.VMEM((2, CHIPS, 8, OWNED), jnp.float32),
            pltpu.VMEM((WIDTH, OWNED), jnp.float32),
            dma((7,)),
            dma((2, 2 * CHIPS)),
            dma((2, 2 * CHIPS)),
            dma((2, CHIPS)),
            dma((2, CHIPS)),
            dma((2, CHIPS)),
            dma((2, CHIPS)),
            dma((2, CHIPS)),
            dma((2, CHIPS)),
            dma((3,)),
            dma((3,)),
        ],
        compiler_params=pltpu.CompilerParams(
            collective_id=0, has_side_effects=True, vmem_limit_bytes=60 * 1024 * 1024
        ),
    )(slots, u_factors, v_factors, ratings[0, 0], u_noise, v_noise)


def solution(mesh):
    placed = (
        P(("user", "item"), None),
        P(("item", "user"), None),
        P("user", "item", None, None, None, None),
        P("user", "item", None, None),
        P("user", "item", None, None),
        P("user", "item", None),
        P(None, ("user", "item"), None),
        P(None, ("item", "user"), None),
    )
    return jax.shard_map(
        body,
        mesh=mesh,
        in_specs=placed,
        out_specs=(P(("user", "item"), None), P(("item", "user"), None)),
        check_vma=False,
    )
```

time: 741 us -> 103 us (0.14)
  waiting for transfers between devices: 547 us -> 0 us
  Pallas kernels: 0 us -> 94.9 us
  other arithmetic: 86 us -> 2.33 us
  local copies, waits for them, and re-layouts: 46.8 us -> 3.79 us
  matrix products: 33.4 us -> 0 us
  between operations: 15.1 us -> 0.65 us
  starting transfers between devices: 8.14 us -> 0 us
    reduce_scatter x2 -> x0, waiting for transfers between devices: 490 us -> none  [body(): owned = lax.psum_scatter(grad_item, 'user', scatter_dimension=0, tiled=True)]
    pallas_call x0 -> x1, Pallas kernels: none -> 94.9 us  [body(): pl.pallas_call(kernel, out_shape=(jax.ShapeDtypeStruct(u_factors.shape, j...]
    scatter-add x14 -> x0, other arithmetic: 67.1 us -> none  [the longest x7 36.6 us: advance(): grad_item.at[cols_now]]
    all_gather x2 -> x0, waiting for transfers between devices: 49.7 us -> none  [body(): lax.all_gather(item_master.astype(jnp.bfloat16), 'user', axis=0, tiled=True)]
    dot_general x21 -> x0, matrix products: 33.4 us -> none  [the longest x7 12.8 us: advance(): jnp.einsum('tab,tak->tbk', misfit, user_part, preferred_element_type=jnp....]
    gather x14 -> x0, local copies, waits for them, and re-layouts: 19.7 us -> none  [the longest x7 15.4 us: advance(): item_part = item_tiles[cols_now]]
    squeeze x1 -> x0, local copies, waits for them, and re-layouts: 10.7 us -> none  [body(): ratings[0, 0, section]]
    another operation x4 -> x0, local copies, waits for them, and re-layouts: 8.08 us -> none
  transfers between devices with their start and end apart: 6 -> 0, of which waited for: 5 -> 0; matrix products, arithmetic and copies ran while one was open for 3% -> 0% of each run, Pallas kernels for 0% -> 0%
where the time goes in v2:
time: 103 us; the launch traced here: 102 us
  Pallas kernels  94.9 us (92%)
  local copies, waits for them, and re-layouts  3.79 us (4%)
  other arithmetic  2.33 us (2%)
    pallas_call x1, Pallas kernels, body(): pl.pallas_call(kernel, out_shape=(jax.ShapeDtypeStruct(u_factors.shape, j...  94.9 us
    unnamed x4, local copies, waits for them, and re-layouts  3.79 us

profile of v2, /device:TPU:0, one launch (start us, length us, event | category | flops | bytes accessed | tf_op | source)
XLA Modules:
  0.0 101.7 jit_solution(1400067764064971413)
XLA Ops:
  0.6 0.7 iota_compare_fusion.1
  1.4 0.7 add_bitcast_fusion
  2.1 0.9 select_reduce_fusion.refs_0_
  3.0 94.9 %shard_map.95 = (f32[2048,256]{1,0:T(8,128)}, f32[256,256]{1,0:T(8,128)}) custom-call(s32[2,512]{1,0:T(2,128)} %select_reduce_fusion.refs_0_, f32[2048,256]{1,0:T(8,128)} %refs_1_.1, f32[256,256]{1,0:T(8,128)} %refs_2_.1, bf16[2,224,128,128]{3,2,1,0:T(8,128)(2,1)} %bitcast.4, bf16[2,2048,256]{2,1,0:T(8,128)(2,1)} %refs_4_.1, bf16[2,256,256]{2,1,0:T(8,128)(2,1)} %refs_5_.1), custom_call_target="tpu_custom_call" | custom-call | tf_op jit(solution)/shard_map/pallas_call | solution.py:297
  97.9 0.0 copy-start
  97.9 3.1 %copy.12 = f32[2048,256]{1,0:T(8,128)} copy(f32[2048,256]{1,0:T(8,128)} %get-tuple-element.4) | data formatting | bytes 4194304
  101.0 0.0 copy-done
  101.0 0.7 copy.13
Async XLA Ops:
  97.9 3.1 %copy-start = (f32[256,256]{1,0:T(8,128)S(1)}, f32[256,256]{1,0:T(8,128)}, u32[]{:S(2)}) copy-start(f32[256,256]{1,0:T(8,128)} %get-tuple-element.5) | copy-start | bytes 786436

commit v3 on v2

v3 whole, which is shorter than its diff:
```python
import math

import jax
import jax.numpy as jnp
from jax import lax
from jax.experimental import pallas as pl
from jax.experimental.pallas import tpu as pltpu
from jax.sharding import PartitionSpec as P

HALF_STEP = 0.002
ROOT_STEP = math.sqrt(0.004)
PRIOR = 25.0
LEVELS = 32767.0
MESH = pl.DeviceIdType.MESH

TILE = 128
WIDTH = 256
BLOCK = 2048
OWNED = 256
CHIPS = 8
ITEM_PEERS = 8
BAND = 256
BANDS = BLOCK // BAND


VISIT_Y = (0, 0, 1, 0, 1, 1, 1, 0)
VISIT_X = (0, 3, 0, 2, 3, 2, 1, 1)
SWAP = 6


def pick(o, table):
    total = 0
    for k, value in enumerate(table):
        if value:
            total = total + jnp.where(o == k, value, 0)
    return total


def offset(chip, dy, dx):
    return lax.rem(chip // 4 + dy, 2) * 4 + lax.rem(lax.rem(chip, 4) + 4 + dx, 4)


def visit(o, chip):
    return offset(chip, pick(o, VISIT_Y), pick(o, VISIT_X))


def visitor(o, chip):
    return offset(chip, pick(o, VISIT_Y), -pick(o, VISIT_X))


def whole_kernel(
    power,
    slots,
    u_hbm,
    v_hbm,
    rating_hbm,
    un_hbm,
    vn_hbm,
    uout_hbm,
    vout_hbm,
    ratings_0,
    ratings_1,
    u_now,
    u_bf,
    u_turned,
    grad_u,
    u_noise,
    v_now,
    v_noise,
    noise_home,
    v_bf,
    group,
    misfit_a,
    misfit_b,
    grad_v,
    from_twin,
    packed,
    scales,
    packed_in,
    scales_in,
    total,
    load_sem,
    ag_send,
    ag_recv,
    twin_send,
    twin_recv,
    q_send,
    q_recv,
    s_send,
    s_recv,
    hop_send,
    hop_recv,
):
    user = lax.axis_index("user")
    item = lax.axis_index("item")
    chip = user // 2
    core = lax.rem(user, 2)
    twin = (chip * 2 + 1 - core, item)
    across = offset(chip, 1, 0) * 2 + core
    next_item = lax.rem(item + 1, ITEM_PEERS)
    last_item = lax.rem(item + ITEM_PEERS - 1, ITEM_PEERS)
    onward = (across, next_item)
    back = (across, last_item)

    def seen(o):
        return (visit(o, chip) * 2 + core, item)

    def at(dy, dx):
        return (offset(chip, dy, dx) * 2 + core, item)

    ratings = (ratings_0, ratings_1)
    load_v = pltpu.make_async_copy(v_hbm, v_now, load_sem.at[0])
    load_u = pltpu.make_async_copy(u_hbm, u_now, load_sem.at[1])
    load_0 = pltpu.make_async_copy(rating_hbm.at[0], ratings_0, load_sem.at[2])
    load_un = pltpu.make_async_copy(un_hbm, u_noise, load_sem.at[3])
    load_vn = pltpu.make_async_copy(vn_hbm, v_noise, load_sem.at[4])
    load_1 = pltpu.make_async_copy(rating_hbm.at[1], ratings_1, load_sem.at[5])
    barrier = pltpu.get_barrier_semaphore()
    for peer in [onward, back, (user, next_item), (user, last_item), twin]:
        pl.semaphore_signal(barrier, inc=1, device_id=peer, device_id_type=MESH)

    def greet(o, _):
        pl.semaphore_signal(barrier, inc=1, device_id=seen(CHIPS - o), device_id_type=MESH)
        return 0

    lax.fori_loop(1, CHIPS, greet, 0)
    load_v.start()
    load_u.start()
    load_0.start()
    load_vn.start()

    def remote(src, dst, send, recv, device):
        return pltpu.make_async_remote_copy(
            src_ref=src, dst_ref=dst, send_sem=send, recv_sem=recv, device_id=device, device_id_type=MESH
        )

    noise_copy = remote(v_noise.at[1], noise_home, hop_send.at[1], hop_recv.at[1], (user, last_item))

    def ag_copy(s, owner, lane, device):
        at = group.at[s, owner]
        return remote(at, at, ag_send.at[s, lane], ag_recv.at[s, owner], device)

    def spread(s):
        ag_copy(s, user, 1, at(0, 1)).start()
        ag_copy(s, user, 2, at(0, -1)).start()
        ag_copy(s, user, 3, at(1, 0)).start()
        ag_copy(s, user, 0, twin).start()

    def pass_on(s, order, dy, dx):
        owner = offset(chip, dy, dx) * 2 + core
        ag_copy(s, owner, 0, twin).wait_recv()
        ag_copy(s, owner, CHIPS + order, twin).start()
        if (dy, dx) == (1, 0):
            ag_copy(s, owner, 5, at(0, 1)).start()
            ag_copy(s, owner, 6, at(0, -1)).start()
        if (dy, dx) == (0, 2):
            ag_copy(s, owner, 7, at(1, 0)).start()
        if (dy, dx) == (0, -1):

            @pl.when(core == 0)
            def _():
                ag_copy(s, owner, 4, at(0, 1)).start()

        if (dy, dx) == (0, 1):

            @pl.when(core == 1)
            def _():
                ag_copy(s, owner, 4, at(0, -1)).start()

    def twin_copy(s, o):
        return remote(
            grad_v.at[o, 1 - core], from_twin.at[s, o], twin_send.at[s, o], twin_recv.at[s, o], twin
        )

    def q_copy(s, o, slot):
        return remote(packed.at[o], packed_in.at[s, slot], q_send.at[s, o], q_recv.at[s, slot], seen(o))

    def s_copy(s, o, slot):
        return remote(scales.at[o], scales_in.at[s, slot], s_send.at[s, o], s_recv.at[s, slot], seen(o))

    def prepare(s):
        def one(b, _):
            rows = pl.ds(pl.multiple_of(b * BAND, BAND), BAND)
            now = u_now[rows, :]
            if s > 0:
                now = (
                    now
                    + HALF_STEP * (power * grad_u[rows, :] - PRIOR * now)
                    + ROOT_STEP * u_noise[s - 1, rows, :].astype(jnp.float32)
                )
                u_now[rows, :] = now
            if s < 2:
                u_bf[rows, :] = now.astype(jnp.bfloat16)
                u_turned[:, rows] = now.T.astype(jnp.bfloat16)
                grad_u[rows, :] = jnp.zeros((BAND, WIDTH), jnp.float32)
            return 0

        lax.fori_loop(0, BANDS, one, 0)

    def predict(s, owner, misfit):
        items = group[s, owner]
        tiles = 2 * (owner if s == 0 else lax.rem(owner + 8, 16))
        for b in range(BANDS):
            rows = pl.ds(b * BAND, BAND)
            predicted = lax.dot_general(
                u_bf[rows, :], items, (((1,), (1,)), ((), ())), preferred_element_type=jnp.float32
            )
            for i in range(BAND // TILE):
                for j in range(OWNED // TILE):
                    at = slots[s, (b * (BAND // TILE) + i) * 32 + tiles + j]
                    rating = ratings[s][jnp.maximum(at, 0)].astype(jnp.float32)
                    part = predicted[i * TILE : (i + 1) * TILE, j * TILE : (j + 1) * TILE]
                    misfit[pl.ds(b * BAND + i * TILE, TILE), pl.ds(j * TILE, TILE)] = jnp.where(
                        at >= 0, rating - part, 0.0
                    ).astype(jnp.bfloat16)

    def grads(s, o, owner, half, misfit):
        items = group[s, owner]
        for b in range(BANDS):
            rows = pl.ds(b * BAND, BAND)
            grad_u[rows, :] += jnp.dot(misfit[rows, :], items, preferred_element_type=jnp.float32)
        grad_v[o, half] = jnp.dot(u_turned[...], misfit[...], preferred_element_type=jnp.float32)

    def coded(term):
        peak = jnp.max(jnp.abs(term), axis=0, keepdims=True)
        inverse = jnp.where(peak > 1e-30, LEVELS / jnp.maximum(peak, 1e-30), 0.0)
        code = jnp.round(term * inverse).astype(jnp.int32).astype(jnp.int16)
        return code, jnp.broadcast_to(peak * (1.0 / LEVELS), (8, OWNED))

    def decoded(code, step):
        return code.astype(jnp.int32).astype(jnp.float32) * step[0:1, :]

    def finish(s, o):
        twin_copy(s, o).wait_recv()
        packed[o], scales[o] = coded(grad_v[o, core] + from_twin[s, o])
        q_copy(s, o, chip).start()
        s_copy(s, o, chip).start()

    def half_of(o, second):
        first = jnp.where(o < SWAP, core, 1 - core)
        return 1 - first if second else first

    def owner_of(o, second):
        return visit(o, chip) * 2 + half_of(o, second)

    def await_twin(s, o):
        ag_copy(s, visit(o, chip) * 2 + 1 - core, 0, twin).wait_recv()

    def first_block(s, o):
        @pl.when(o < SWAP)
        def _():
            await_twin(s, o)

        predict(s, owner_of(o, True), misfit_b)
        grads(s, o, owner_of(o, False), half_of(o, False), misfit_a)

        @pl.when(o >= SWAP)
        def _():
            twin_copy(s, o).start()

        @pl.when(o > 1)
        def _():
            finish(s, o - 1)

    def section(s):
        predict(s, user, misfit_a)

        def meet(o, _):
            first_block(s, o)

            @pl.when(o == 0)
            def _():
                pass_on(s, 1, 0, -1)

            @pl.when(o == 2)
            def _():
                pass_on(s, 6, 0, 2)

            @pl.when(o == 4)
            def _():
                pass_on(s, 7, 1, 2)

            @pl.when(o + 1 >= SWAP)
            def _():
                await_twin(s, o + 1)

            predict(s, owner_of(o + 1, False), misfit_a)
            grads(s, o, owner_of(o, True), half_of(o, True), misfit_b)

            @pl.when(o < SWAP)
            def _():
                twin_copy(s, o).start()

            @pl.when(o == 0)
            def _():
                pass_on(s, 2, 1, 0)
                pass_on(s, 3, 0, 1)

            @pl.when(o == 2)
            def _():
                pass_on(s, 4, 1, -1)
                pass_on(s, 5, 1, 1)

            if s == 0:

                @pl.when(o == 1)
                def _():
                    load_1.start()
                    load_un.start()

                @pl.when(o == 5)
                def _():
                    noise_copy.start()

            return 0

        lax.fori_loop(0, CHIPS - 1, meet, 0)
        last = CHIPS - 1
        first_block(s, last)
        grads(s, last, owner_of(last, True), half_of(last, True), misfit_b)
        finish(s, last)

    def own_sum(s):
        twin_copy(s, 0).wait_recv()
        total[...] = grad_v[0, core] + from_twin[s, 0]

        def add(o, _):
            slot = visitor(o, chip)
            q_copy(s, o, slot).wait_recv()
            s_copy(s, o, slot).wait_recv()
            total[...] += decoded(packed_in[s, slot], scales_in[s, slot])
            return 0

        lax.fori_loop(1, CHIPS, add, 0)

    def settle(s):
        ag_copy(s, user, 0, twin).wait_send()
        twin_copy(s, 0).wait_send()

        def one(o, _):
            ag_copy(s, user, o, twin).wait_send()
            ag_copy(s, user, CHIPS + o, twin).wait_send()
            twin_copy(s, o).wait_send()
            q_copy(s, o, chip).wait_send()
            s_copy(s, o, chip).wait_send()
            return 0

        lax.fori_loop(1, CHIPS, one, 0)

    load_u.wait()
    prepare(0)
    load_v.wait()
    group[0, user] = v_now[...].astype(jnp.bfloat16)
    load_vn.wait()
    load_0.wait()
    pl.semaphore_wait(barrier, 5 + CHIPS - 1)
    spread(0)
    section(0)
    load_un.wait()
    prepare(1)
    own_sum(0)
    now = v_now[...]
    now = now + HALF_STEP * (power * total[...].T - PRIOR * now) + ROOT_STEP * v_noise[0].astype(jnp.float32)
    v_bf[...] = now.astype(jnp.bfloat16)
    hop = remote(v_bf, group.at[1, across], hop_send.at[0], hop_recv.at[0], onward)
    hop.start()
    v_now[...] = now
    settle(0)
    hop.wait_recv()

    spread(1)
    load_1.wait()
    section(1)
    prepare(2)
    store_u = pltpu.make_async_copy(u_now, uout_hbm, load_sem.at[1])
    store_u.start()
    own_sum(1)
    packed[0], scales[0] = coded(total[...])
    home = offset(chip, 1, 0)
    home_q = remote(packed.at[0], packed_in.at[1, home], hop_send.at[2], hop_recv.at[2], back)
    home_s = remote(scales.at[0], scales_in.at[1, home], hop_send.at[3], hop_recv.at[3], back)
    home_q.start()
    home_s.start()
    settle(1)
    hop.wait_send()
    noise_copy.wait()
    now = v_now[...]
    now = now - HALF_STEP * PRIOR * now + ROOT_STEP * noise_home[...].astype(jnp.float32)
    home_q.wait()
    home_s.wait()
    v_now[...] = now + HALF_STEP * power * decoded(packed_in[1, chip], scales_in[1, chip]).T
    store_v = pltpu.make_async_copy(v_now, vout_hbm, load_sem.at[0])
    store_v.start()
    store_u.wait()
    store_v.wait()


def slot_map(rows, cols, counts):
    sections, listed = rows.shape
    cell = jnp.arange(512, dtype=jnp.int32)[None, :, None]
    slot = jnp.arange(listed, dtype=jnp.int32)
    hit = (rows * 32 + cols)[:, None, :] == cell
    live = (slot[None, :] < counts[:, None])[:, None, :]
    return jnp.max(jnp.where(hit & live, slot[None, None, :], -1), axis=2)


def body(u_factors, v_factors, ratings, tile_rows, tile_cols, tile_counts, u_noise, v_noise):
    slots = slot_map(tile_rows[0, 0], tile_cols[0, 0], tile_counts[0, 0])
    listed = ratings.shape[3]
    power = float(lax.axis_size("item"))
    anywhere = pl.BlockSpec(memory_space=pl.ANY)
    dma = pltpu.SemaphoreType.DMA

    def kernel(*refs):
        whole_kernel(power, *refs)

    return pl.pallas_call(
        kernel,
        out_shape=(
            jax.ShapeDtypeStruct(u_factors.shape, jnp.float32),
            jax.ShapeDtypeStruct(v_factors.shape, jnp.float32),
        ),
        in_specs=[pl.BlockSpec(memory_space=pltpu.SMEM)] + [anywhere] * 5,
        out_specs=(anywhere, anywhere),
        scratch_shapes=[
            pltpu.VMEM((listed, TILE, TILE), jnp.bfloat16),
            pltpu.VMEM((listed, TILE, TILE), jnp.bfloat16),
            pltpu.VMEM((BLOCK, WIDTH), jnp.float32),
            pltpu.VMEM((BLOCK, WIDTH), jnp.bfloat16),
            pltpu.VMEM((WIDTH, BLOCK), jnp.bfloat16),
            pltpu.VMEM((BLOCK, WIDTH), jnp.float32),
            pltpu.VMEM((2, BLOCK, WIDTH), jnp.bfloat16),
            pltpu.VMEM((OWNED, WIDTH), jnp.float32),
            pltpu.VMEM((2, OWNED, WIDTH), jnp.bfloat16),
            pltpu.VMEM((OWNED, WIDTH), jnp.bfloat16),
            pltpu.VMEM((OWNED, WIDTH), jnp.bfloat16),
            pltpu.VMEM((2, 2 * CHIPS, OWNED, WIDTH), jnp.bfloat16),
            pltpu.VMEM((BLOCK, OWNED), jnp.bfloat16),
            pltpu.VMEM((BLOCK, OWNED), jnp.bfloat16),
            pltpu.VMEM((CHIPS, 2, WIDTH, OWNED), jnp.float32),
            pltpu.VMEM((2, CHIPS, WIDTH, OWNED), jnp.float32),
            pltpu.VMEM((CHIPS, WIDTH, OWNED), jnp.int16),
            pltpu.VMEM((CHIPS, 8, OWNED), jnp.float32),
            pltpu.VMEM((2, CHIPS, WIDTH, OWNED), jnp.int16),
            pltpu.VMEM((2, CHIPS, 8, OWNED), jnp.float32),
            pltpu.VMEM((WIDTH, OWNED), jnp.float32),
            dma((6,)),
            dma((2, 2 * CHIPS)),
            dma((2, 2 * CHIPS)),
            dma((2, CHIPS)),
            dma((2, CHIPS)),
            dma((2, CHIPS)),
            dma((2, CHIPS)),
            dma((2, CHIPS)),
            dma((2, CHIPS)),
            dma((4,)),
            dma((4,)),
        ],
        compiler_params=pltpu.CompilerParams(
            collective_id=0, has_side_effects=True, vmem_limit_bytes=60 * 1024 * 1024
        ),
    )(slots, u_factors, v_factors, ratings[0, 0], u_noise, v_noise)


def solution(mesh):
    placed = (
        P(("user", "item"), None),
        P(("item", "user"), None),
        P("user", "item", None, None, None, None),
        P("user", "item", None, None),
        P("user", "item", None, None),
        P("user", "item", None),
        P(None, ("user", "item"), None),
        P(None, ("item", "user"), None),
    )
    return jax.shard_map(
        body,
        mesh=mesh,
        in_specs=placed,
        out_specs=(P(("user", "item"), None), P(("item", "user"), None)),
        check_vma=False,
    )
```

time: 103 us -> 94.8 us (0.920)
  Pallas kernels: 94.9 us -> 87.4 us
    pallas_call x1, Pallas kernels: 94.9 us -> 87.4 us  [body(): pl.pallas_call(kernel, out_shape=(jax.ShapeDtypeStruct(u_factors.shape, j...]
where the time goes in v3:
time: 94.8 us; the launch traced here: 94.2 us
  Pallas kernels  87.4 us (92%)
  local copies, waits for them, and re-layouts  3.79 us (4%)
  other arithmetic  2.33 us (2%)
    pallas_call x1, Pallas kernels, body(): pl.pallas_call(kernel, out_shape=(jax.ShapeDtypeStruct(u_factors.shape, j...  87.4 us
    unnamed x4, local copies, waits for them, and re-layouts  3.79 us

profile of v3, /device:TPU:0, one launch (start us, length us, event | category | flops | bytes accessed | tf_op | source)
XLA Modules:
  0.0 94.2 jit_solution(6707433878260377822)
XLA Ops:
  0.6 0.7 iota_compare_fusion.1
  1.4 0.7 add_bitcast_fusion
  2.1 0.9 select_reduce_fusion.refs_0_
  3.0 87.4 %shard_map.95 = (f32[2048,256]{1,0:T(8,128)}, f32[256,256]{1,0:T(8,128)}) custom-call(s32[2,512]{1,0:T(2,128)} %select_reduce_fusion.refs_0_, f32[2048,256]{1,0:T(8,128)} %refs_1_.1, f32[256,256]{1,0:T(8,128)} %refs_2_.1, bf16[2,224,128,128]{3,2,1,0:T(8,128)(2,1)} %bitcast.4, bf16[2,2048,256]{2,1,0:T(8,128)(2,1)} %refs_4_.1, bf16[2,256,256]{2,1,0:T(8,128)(2,1)} %refs_5_.1), custom_call_target="tpu_custom_call" | custom-call | tf_op jit(solution)/shard_map/pallas_call | solution.py:417
  90.4 0.0 copy-start
  90.4 3.1 %copy.12 = f32[2048,256]{1,0:T(8,128)} copy(f32[2048,256]{1,0:T(8,128)} %get-tuple-element.4) | data formatting | bytes 4194304
  93.5 0.0 copy-done
  93.5 0.7 copy.13
Async XLA Ops:
  90.4 3.1 %copy-start = (f32[256,256]{1,0:T(8,128)S(1)}, f32[256,256]{1,0:T(8,128)}, u32[]{:S(2)}) copy-start(f32[256,256]{1,0:T(8,128)} %get-tuple-element.5) | copy-start | bytes 786436

commit v4 on v3

--- a/solution.py
+++ b/solution.py
@@ -24,7 +24,7 @@
 
 
 VISIT_Y = (0, 0, 1, 0, 1, 1, 1, 0)
-VISIT_X = (0, 3, 0, 2, 3, 2, 1, 1)
+VISIT_X = (0, 1, 0, 2, 1, 2, 3, 3)
 SWAP = 6
 
 
@@ -141,10 +141,10 @@
         return remote(at, at, ag_send.at[s, lane], ag_recv.at[s, owner], device)
 
     def spread(s):
+        ag_copy(s, user, 0, twin).start()
         ag_copy(s, user, 1, at(0, 1)).start()
         ag_copy(s, user, 2, at(0, -1)).start()
         ag_copy(s, user, 3, at(1, 0)).start()
-        ag_copy(s, user, 0, twin).start()
 
     def pass_on(s, order, dy, dx):
         owner = offset(chip, dy, dx) * 2 + core
@@ -270,7 +270,7 @@
 
             @pl.when(o == 0)
             def _():
-                pass_on(s, 1, 0, -1)
+                pass_on(s, 3, 0, 1)
 
             @pl.when(o == 2)
             def _():
@@ -294,12 +294,12 @@
             @pl.when(o == 0)
             def _():
                 pass_on(s, 2, 1, 0)
-                pass_on(s, 3, 0, 1)
+                pass_on(s, 1, 0, -1)
 
             @pl.when(o == 2)
             def _():
+                pass_on(s, 5, 1, 1)
                 pass_on(s, 4, 1, -1)
-                pass_on(s, 5, 1, 1)
 
             if s == 0:
 
@@ -396,12 +396,10 @@
 
 
 def slot_map(rows, cols, counts):
-    sections, listed = rows.shape
-    cell = jnp.arange(512, dtype=jnp.int32)[None, :, None]
-    slot = jnp.arange(listed, dtype=jnp.int32)
-    hit = (rows * 32 + cols)[:, None, :] == cell
-    live = (slot[None, :] < counts[:, None])[:, None, :]
-    return jnp.max(jnp.where(hit & live, slot[None, None, :], -1), axis=2)
+    slot = jnp.arange(rows.shape[1], dtype=jnp.int32)
+    cell = jnp.arange(512, dtype=jnp.int32)
+    held = jnp.where(slot < counts[:, None], rows * 32 + cols, -1)
+    return jnp.max(jnp.where(held[:, None, :] == cell[None, :, None], slot, -1), axis=2)
 
 
 def body(u_factors, v_factors, ratings, tile_rows, tile_cols, tile_counts, u_noise, v_noise):

time: 94.8 us -> 93.5 us (0.986)
  no operation moved by 1% of the time
where the time goes in v4:
time: 93.5 us; the launch traced here: 93.3 us
  Pallas kernels  87.3 us (93%)
  local copies, waits for them, and re-layouts  3.79 us (4%)
  other arithmetic  1.57 us (2%)
    pallas_call x1, Pallas kernels, body(): pl.pallas_call(kernel, out_shape=(jax.ShapeDtypeStruct(u_factors.shape, j...  87.3 us
    unnamed x4, local copies, waits for them, and re-layouts  3.79 us

profile of v4, /device:TPU:0, one launch (start us, length us, event | category | flops | bytes accessed | tf_op | source)
XLA Modules:
  0.0 93.3 jit_solution(15090501927642740144)
XLA Ops:
  0.6 0.8 compare_select_fusion
  1.4 0.8 select_reduce_fusion.refs_0_
  2.2 87.3 %shard_map.95 = (f32[2048,256]{1,0:T(8,128)}, f32[256,256]{1,0:T(8,128)}) custom-call(s32[2,512]{1,0:T(2,128)} %select_reduce_fusion.refs_0_, f32[2048,256]{1,0:T(8,128)} %refs_1_.1, f32[256,256]{1,0:T(8,128)} %refs_2_.1, bf16[2,224,128,128]{3,2,1,0:T(8,128)(2,1)} %bitcast.4, bf16[2,2048,256]{2,1,0:T(8,128)(2,1)} %refs_4_.1, bf16[2,256,256]{2,1,0:T(8,128)(2,1)} %refs_5_.1), custom_call_target="tpu_custom_call" | custom-call | tf_op jit(solution)/shard_map/pallas_call | solution.py:415
  89.5 0.0 copy-start
  89.5 3.1 %copy.12 = f32[2048,256]{1,0:T(8,128)} copy(f32[2048,256]{1,0:T(8,128)} %get-tuple-element.4) | data formatting | bytes 4194304
  92.6 0.0 copy-done
  92.6 0.7 copy.13
Async XLA Ops:
  89.5 3.1 %copy-start = (f32[256,256]{1,0:T(8,128)S(1)}, f32[256,256]{1,0:T(8,128)}, u32[]{:S(2)}) copy-start(f32[256,256]{1,0:T(8,128)} %get-tuple-element.5) | copy-start | bytes 786436
